TPU v7x, 32 devices: a whole 2x2x4 slice. The times are simulated.
32 devices in a mesh: dp: 4 (over x, core), ctx: 8 (over z, y).
Axes of the slice: x: 2, y: 2, z: 4, core: 2. Of those that a mesh axis runs over, the one named last changes fastest.
Arguments:
- queries: bfloat16 [4, 2048, 1024], P('dp', 'ctx'), may hold values from -4.5 to 4.5
- keys: bfloat16 [4, 2048, 1024], P('dp', 'ctx'), may hold values from -4.5 to 4.5
- values: bfloat16 [4, 2048, 1024], P('dp', 'ctx'), may hold values from -6 to 6
- out_grad: bfloat16 [4, 2048, 2048], P('dp', 'ctx'), may hold values from -6 to 6
- chosen: int32 [4, 8], P('dp'), may hold values from -1 to 15, as said below
- proj: bfloat16 [1024, 2048], P('ctx', 'dp'), may hold values from -0.1875 to 0.1875
Outputs:
- attn_out: bfloat16 [4, 2048, 2048], P('dp', 'ctx')
- q_grad: bfloat16 [4, 2048, 1024], P('dp', 'ctx')
- k_grad: bfloat16 [4, 2048, 1024], P('dp', 'ctx')
- v_grad: bfloat16 [4, 2048, 1024], P('dp', 'ctx')
- proj_grad: float32 [1024, 2048], P('ctx', 'dp')
Inputs may be any that keep to these rules, and one draw needn't show every extreme that they name: chosen[d, c] is -1 or the index pos // 128 of one of the blocks that ctx index c stores (position spans c and 15 - c, of 1 block each); every sequence has one or more entries that are not -1.
All inputs are finite; a program needn't handle non-finite values.
Results may differ from a plain program's by a relative error of at most 0.023.
Values may be sent and summed in bfloat16 or wider, within the bound.
A program may use at most 192 MiB of HBM per device.

v0:
```python
import math
import jax
import jax.numpy as jnp
from jax import lax
from jax.sharding import PartitionSpec as P

BLOCK = 128


def cross_dot(left_op, right_op):
    return lax.dot_general(
        left_op, right_op, (((1,), (1,)), ((), ())), preferred_element_type=jnp.float32
    )


def inner_dot(left_op, right_op):
    return lax.dot_general(
        left_op, right_op, (((0,), (0,)), ((), ())), preferred_element_type=jnp.float32
    )


def head_probs(
    query_block,
    query_pos,
    query_live,
    query_ids,
    heads_k,
    slot_pos,
    slot_live,
    slot_ids,
    score_scale,
):
    scores = cross_dot(query_block, heads_k) * score_scale
    allowed = query_live[:, None] & slot_live[None, :] & (
        slot_pos[None, :] <= query_pos[:, None]
    ) | (query_ids[:, None] == slot_ids[None, :])
    masked = jnp.where(allowed, scores, -1e30)
    row_max = jnp.max(masked, axis=1, keepdims=True)
    exp_terms = jnp.where(allowed, jnp.exp(masked - row_max), 0.0)
    return exp_terms / jnp.sum(exp_terms, axis=1, keepdims=True)


def shards(queries, keys, values, out_grad, chosen, proj):
    ctx_count = lax.axis_size("ctx")
    ctx_index = lax.axis_index("ctx")
    tokens = queries.shape[1]
    half_rows = tokens // 2
    block_rows = BLOCK
    picked = chosen[0]
    own_pick = lax.dynamic_index_in_dim(picked, ctx_index, 0, keepdims=False)
    own_live = own_pick >= 0
    first_pos = jnp.where(own_live, own_pick, 0) * block_rows
    local_row = jnp.where(
        first_pos // half_rows == ctx_index,
        first_pos % half_rows,
        half_rows + first_pos % half_rows,
    )
    row_start = jnp.where(own_live, local_row, 0)

    def take_rows(source):
        slot_block = lax.dynamic_slice_in_dim(source[0], row_start, block_rows, 0)
        return jnp.where(own_live, slot_block, jnp.zeros((), source.dtype))

    def place_rows(slot_block, template):
        return lax.dynamic_update_slice_in_dim(
            jnp.zeros(template.shape, jnp.bfloat16), slot_block[None], row_start, 1
        )

    q_slot = take_rows(queries)
    k_slot = take_rows(keys)
    v_slot = take_rows(values)
    g_slot = take_rows(out_grad)
    heads_q, heads_k, heads_v = (
        lax.all_to_all(q_slot, "ctx", split_axis=1, concat_axis=0, tiled=True),
        lax.all_to_all(k_slot, "ctx", split_axis=1, concat_axis=0, tiled=True),
        lax.all_to_all(v_slot, "ctx", split_axis=1, concat_axis=0, tiled=True),
    )
    slot_count = ctx_count * block_rows
    offsets = jnp.arange(block_rows, dtype=jnp.int32)
    safe_pick = jnp.where(picked >= 0, picked, 0)
    slot_pos = (safe_pick[:, None] * block_rows + offsets[None, :]).reshape(slot_count)
    slot_live = jnp.repeat(picked >= 0, block_rows)
    slot_ids = jnp.arange(slot_count, dtype=jnp.int32)
    head_dim = heads_q.shape[1]
    score_scale = 1.0 / math.sqrt(head_dim)
    step_rows = min(512, slot_count)
    step_count = slot_count // step_rows
    attn_parts = []
    prob_store = []
    prob_b_store = []
    for step_index in range(step_count):
        row_low = step_index * step_rows
        window = slice(row_low, row_low + step_rows)
        attn_prob = head_probs(
            heads_q[window],
            slot_pos[window],
            slot_live[window],
            slot_ids[window],
            heads_k,
            slot_pos,
            slot_live,
            slot_ids,
            score_scale,
        )
        prob_b = attn_prob.astype(jnp.bfloat16)
        prob_store.append(attn_prob)
        prob_b_store.append(prob_b)
        attn_parts.append(
            jnp.dot(prob_b, heads_v, preferred_element_type=jnp.float32).astype(jnp.bfloat16)
        )
    attn_heads = jnp.concatenate(attn_parts, 0)
    attn_local = lax.all_to_all(attn_heads, "ctx", split_axis=0, concat_axis=1, tiled=True)
    head_rows = lax.all_gather(proj, "dp", axis=1, tiled=True)
    full_proj = lax.all_gather(head_rows, "ctx", axis=0, tiled=True)
    mixed = jnp.dot(attn_local, full_proj, preferred_element_type=jnp.float32).astype(jnp.bfloat16)
    attn_out = place_rows(mixed, out_grad)
    part_rows = lax.all_gather(g_slot, "ctx", axis=0, tiled=True)
    weight_term = inner_dot(attn_heads, part_rows)
    rows_grad = cross_dot(part_rows, head_rows)
    weight_term, rows_grad = (weight_term, rows_grad)
    attn_grad = rows_grad.astype(jnp.bfloat16)
    proj_grad = lax.psum_scatter(weight_term, "dp", scatter_dimension=1, tiled=True)
    key_grad = jnp.zeros((slot_count, head_dim), jnp.float32)
    value_grad = jnp.zeros((slot_count, head_dim), jnp.float32)
    query_parts = []
    for step_index in range(step_count):
        row_low = step_index * step_rows
        window = slice(row_low, row_low + step_rows)
        attn_prob = prob_store[step_index]
        prob_b = prob_b_store[step_index]
        grad_block = attn_grad[window]
        row_delta = jnp.sum(
            grad_block.astype(jnp.float32) * attn_heads[window].astype(jnp.float32),
            axis=1,
            keepdims=True,
        )
        score_grad = (attn_prob * (cross_dot(grad_block, heads_v) - row_delta)).astype(jnp.bfloat16)
        query_parts.append(
            (jnp.dot(score_grad, heads_k, preferred_element_type=jnp.float32) * score_scale).astype(
                jnp.bfloat16
            )
        )
        key_grad = key_grad + inner_dot(score_grad, heads_q[window])
        value_grad = value_grad + inner_dot(prob_b, grad_block)
    q_heads_grad = jnp.concatenate(query_parts, 0)
    k_heads_grad = (key_grad * score_scale).astype(jnp.bfloat16)
    v_heads_grad = value_grad.astype(jnp.bfloat16)
    q_back, k_back, v_back = (
        lax.all_to_all(q_heads_grad, "ctx", split_axis=0, concat_axis=1, tiled=True),
        lax.all_to_all(k_heads_grad, "ctx", split_axis=0, concat_axis=1, tiled=True),
        lax.all_to_all(v_heads_grad, "ctx", split_axis=0, concat_axis=1, tiled=True),
    )
    return (
        attn_out,
        place_rows(q_back, queries),
        place_rows(k_back, keys),
        place_rows(v_back, values),
        proj_grad,
    )


def solution(mesh):
    placed = (
        P("dp", "ctx", None),
        P("dp", "ctx", None),
        P("dp", "ctx", None),
        P("dp", "ctx", None),
        P("dp", None),
        P("ctx", "dp"),
    )
    return jax.shard_map(
        shards,
        mesh=mesh,
        in_specs=placed,
        out_specs=(
            P("dp", "ctx", None),
            P("dp", "ctx", None),
            P("dp", "ctx", None),
            P("dp", "ctx", None),
            P("ctx", "dp"),
        ),
        check_vma=False,
    )
```

profile of v0, /device:TPU:0, one launch (start us, length us, event | category | flops | bytes accessed | tf_op | source)
XLA Modules:
  0.0 224.0 jit_solution(12597363358342801564)
XLA Ops:
  9.9 2.0 dynamic-slice_select_fusion
  12.0 10.2 %all_gather.9 = bf16[128,2048]{1,0:T(8,128)(2,1)} all-gather(bf16[128,512]{1,0:T(8,128)(2,1)} %param.11), channel_id=1, replica_groups=mesh['dp'=4,'ctx'=8] {'dp'}, dimensions={1}, use_global_device_ids=true | all-gather | bytes 655360 | tf_op jit(solution)/shard_map/all_gather | solution.py:113
  23.4 5.8 %all-to-all-start.1 = ((bf16[128,8,128]{0,2,1:T(8,128)(2,1)}), bf16[128,8,128]{0,2,1:T(8,128)(2,1)S(1)}, u32[]{:S(2)}, u32[]{:S(2)}) async-start(bf16[128,8,128]{0,2,1:T(8,128)(2,1)} %bitcast.9), calls=%async_computation.1 | async-start | bytes 524288 | tf_op jit(solution)/shard_map/all_to_all | solution.py:75
  30.6 15.6 %all-to-all-done.1 = bf16[128,8,128]{0,2,1:T(8,128)(2,1)S(1)} async-done(((bf16[128,8,128]{0,2,1:T(8,128)(2,1)}), bf16[128,8,128]{0,2,1:T(8,128)(2,1)S(1)}, u32[]{:S(2)}, u32[]{:S(2)}) %all-to-all-start.1) | async-done | bytes 262176 | tf_op jit(solution)/shard_map/all_to_all | solution.py:75
  46.3 3.5 %all-to-all-start = ((bf16[128,8,128]{0,2,1:T(8,128)(2,1)}), bf16[128,8,128]{0,2,1:T(8,128)(2,1)S(1)}, u32[]{:S(2)}, u32[]{:S(2)}) async-start(bf16[128,8,128]{0,2,1:T(8,128)(2,1)} %bitcast.6), calls=%async_computation | async-start | bytes 524288 | tf_op jit(solution)/shard_map/all_to_all | solution.py:74
  50.5 12.3 %all-to-all-done = bf16[128,8,128]{0,2,1:T(8,128)(2,1)S(1)} async-done(((bf16[128,8,128]{0,2,1:T(8,128)(2,1)}), bf16[128,8,128]{0,2,1:T(8,128)(2,1)S(1)}, u32[]{:S(2)}, u32[]{:S(2)}) %all-to-all-start) | async-done | bytes 262176 | tf_op jit(solution)/shard_map/all_to_all | solution.py:74
  62.8 5.5 %all-to-all-start.2 = ((bf16[128,8,128]{0,2,1:T(8,128)(2,1)}), bf16[128,8,128]{0,2,1:T(8,128)(2,1)S(1)}, u32[]{:S(2)}, u32[]{:S(2)}) async-start(bf16[128,8,128]{0,2,1:T(8,128)(2,1)} %bitcast.12), calls=%async_computation.2 | async-start | bytes 524288 | tf_op jit(solution)/shard_map/all_to_all | solution.py:76
  68.9 15.9 %all-to-all-done.2 = bf16[128,8,128]{0,2,1:T(8,128)(2,1)S(1)} async-done(((bf16[128,8,128]{0,2,1:T(8,128)(2,1)}), bf16[128,8,128]{0,2,1:T(8,128)(2,1)S(1)}, u32[]{:S(2)}, u32[]{:S(2)}) %all-to-all-start.2) | async-done | bytes 262176 | tf_op jit(solution)/shard_map/all_to_all | solution.py:76
  87.3 3.0 %fusion.11 = (f32[512]{0:T(512)S(1)}, f32[512]{0:T(512)S(1)}) fusion(f32[512,1024]{1,0:T(8,128)S(1)} %get-tuple-element.21, f32[512]{0:T(512)S(1)} %get-tuple-element.9, s32[512]{0:T(512)S(1)} %slice.46, s32[512]{0:T(512)S(1)} %get-tuple-element.16, s32[1024]{0:T(1024)S(1)} %get-tuple-element.19, pred[1024]{0:T(1024)(128)(4,1)S(1)} %broadcast_bitcast_fusion, ...), kind=kLoop, calls=%fused_computation.22 | loop fusion | flops 10484736 | bytes 4216832 | tf_op jit(solution)/shard_map/reduce_sum | solution.py:40
  90.4 3.8 %fusion.10 = (f32[512,1024]{1,0:T(8,128)}, f32[512,1024]{1,0:T(8,128)S(1)}) fusion(f32[512,1024]{1,0:T(8,128)S(1)} %get-tuple-element.21, f32[512]{0:T(512)S(1)} %get-tuple-element.7, f32[512]{0:T(512)S(1)} %get-tuple-element.9, s32[512]{0:T(512)S(1)} %slice.46, s32[512]{0:T(512)S(1)} %get-tuple-element.16, s32[1024]{0:T(1024)S(1)} %get-tuple-element.19, ...), kind=kLoop, calls=%fused_computation.21 | loop fusion | flops 10485760 | bytes 8411136 | tf_op jit(solution)/shard_map/div | solution.py:40
  94.6 4.0 %all-gather.6.cloned.1.call-done = bf16[1,1024,2048]{2,1,0:T(8,128)(2,1)} async-done(((bf16[1,128,2048]{2,1,0:T(8,128)(2,1)}), bf16[1,1024,2048]{2,1,0:T(8,128)(2,1)}) %all-gather.6.cloned.1.call-update) | async-done | bytes 4194320 | tf_op jit(solution)/shard_map/all_gather | solution.py:117
  98.6 3.7 %fusion.16 = bf16[1024,128]{1,0:T(8,128)(2,1)S(1)} fusion(bf16[128,2048]{1,0:T(8,128)(2,1)} %all_gather.9, bf16[1,1024,2048]{2,1,0:T(8,128)(2,1)} %all-gather.6.cloned.1.call-done), kind=kOutput, calls=%fused_computation.27 | convolution fusion | flops 537001984 | bytes 4980736 | tf_op jit(solution)/shard_map/dot_general | solution.py:11
  104.0 4.0 %all-to-all-start.6 = ((bf16[8,128,128]{2,1,0:T(8,128)(2,1)}), bf16[8,128,128]{2,1,0:T(8,128)(2,1)}, u32[]{:S(2)}, u32[]{:S(2)}) async-start(bf16[8,128,128]{2,1,0:T(8,128)(2,1)} %bitcast.79), calls=%async_computation.6 | async-start | bytes 524288 | tf_op jit(solution)/shard_map/all_to_all | solution.py:151
  108.1 2.3 %multiply_reduce_fusion.1 = (f32[512]{0:T(512)S(1)}, f32[512]{0:T(512)S(1)}, bf16[512,128]{1,0:T(8,128)(2,1)S(1)}) fusion(bf16[1024,128]{1,0:T(8,128)(2,1)S(1)} %fusion.16, bf16[512,128]{1,0:T(8,128)(2,1)S(1)} %convolution_convert_fusion.1, bf16[1024,128]{1,0:T(8,128)(2,1)S(1)} %bitcast.69, f32[512,1024]{1,0:T(8,128)} %get-tuple-element.13), kind=kOutput, calls=%fused_computation.43 | convolution fusion | flops 135330816 | bytes 2887680 | tf_op jit(solution)/shard_map/dot_general | solution.py:109
  117.6 7.5 %all-to-all-done.6 = bf16[8,128,128]{2,1,0:T(8,128)(2,1)} async-done(((bf16[8,128,128]{2,1,0:T(8,128)(2,1)}), bf16[8,128,128]{2,1,0:T(8,128)(2,1)}, u32[]{:S(2)}, u32[]{:S(2)}) %all-to-all-start.6) | async-done | bytes 262176 | tf_op jit(solution)/shard_map/all_to_all | solution.py:151
  125.1 3.6 %all-to-all-start.5 = ((bf16[8,128,128]{2,1,0:T(8,128)(2,1)}), bf16[8,128,128]{2,1,0:T(8,128)(2,1)S(1)}, u32[]{:S(2)}, u32[]{:S(2)}) async-start(bf16[8,128,128]{2,1,0:T(8,128)(2,1)} %bitcast.25), calls=%async_computation.5 | async-start | bytes 524288 | tf_op jit(solution)/shard_map/all_to_all | solution.py:150
  130.3 8.7 %all-to-all-done.5 = bf16[8,128,128]{2,1,0:T(8,128)(2,1)S(1)} async-done(((bf16[8,128,128]{2,1,0:T(8,128)(2,1)}), bf16[8,128,128]{2,1,0:T(8,128)(2,1)S(1)}, u32[]{:S(2)}, u32[]{:S(2)}) %all-to-all-start.5) | async-done | bytes 262176 | tf_op jit(solution)/shard_map/all_to_all | solution.py:150
  139.0 3.5 %all-to-all-start.4 = ((bf16[8,128,128]{2,1,0:T(8,128)(2,1)}), bf16[8,128,128]{2,1,0:T(8,128)(2,1)S(1)}, u32[]{:S(2)}, u32[]{:S(2)}) async-start(bf16[8,128,128]{2,1,0:T(8,128)(2,1)} %bitcast.23), calls=%async_computation.4 | async-start | bytes 524288 | tf_op jit(solution)/shard_map/all_to_all | solution.py:149
  143.4 15.6 %all-to-all-done.4 = bf16[8,128,128]{2,1,0:T(8,128)(2,1)S(1)} async-done(((bf16[8,128,128]{2,1,0:T(8,128)(2,1)}), bf16[8,128,128]{2,1,0:T(8,128)(2,1)S(1)}, u32[]{:S(2)}, u32[]{:S(2)}) %all-to-all-start.4) | async-done | bytes 262176 | tf_op jit(solution)/shard_map/all_to_all | solution.py:149
  159.0 3.7 %all-to-all-start.3 = ((bf16[8,128,128]{1,2,0:T(8,128)(2,1)}), bf16[8,128,128]{1,2,0:T(8,128)(2,1)S(1)}, u32[]{:S(2)}, u32[]{:S(2)}) async-start(bf16[8,128,128]{1,2,0:T(8,128)(2,1)} %copy.27), calls=%async_computation.3 | async-start | bytes 524288 | tf_op jit(solution)/shard_map/all_to_all | solution.py:112
  168.9 21.6 %all-gather.4.cloned.1.call-done = bf16[1024,2048]{1,0:T(8,128)(2,1)} async-done(((bf16[128,2048]{1,0:T(8,128)(2,1)}), bf16[1024,2048]{1,0:T(8,128)(2,1)}) %all-gather.4.cloned.1.call-update) | async-done | bytes 4194320 | tf_op jit(solution)/shard_map/all_gather | solution.py:114
  190.5 2.9 %fusion.4 = bf16[1,128,2048]{2,1,0:T(8,128)(2,1)S(1)} fusion(bf16[128,1024]{0,1:T(8,128)(2,1)S(1)} %bitcast.78, bf16[1024,2048]{1,0:T(8,128)(2,1)} %all-gather.4.cloned.1.call-done), kind=kOutput, calls=%fused_computation.5 | convolution fusion | flops 537133056 | bytes 4980736 | tf_op jit(solution)/shard_map/dot_general | solution.py:115
  193.6 2.5 %dynamic_update_slice.12 = bf16[1,256,2048]{2,1,0:T(8,128)(2,1)S(1)} dynamic-update-slice(bf16[1,256,2048]{2,1,0:T(8,128)(2,1)S(1)} %broadcast_in_dim.59, bf16[1,128,2048]{2,1,0:T(8,128)(2,1)S(1)} %fusion.4, s32[]{:T(128)} %constant.48.clone.1, s32[]{:T(128)S(6)} %select_n.105, s32[]{:T(128)} %constant.48.clone.1) | dynamic-update-slice | bytes 1048580 | tf_op jit(solution)/shard_map/dynamic_update_slice | solution.py:65
  196.1 21.3 %reduce-scatter.2.cloned.1.call-done = f32[128,512]{1,0:T(8,128)} async-done(((f32[128,2048]{1,0:T(8,128)}), f32[128,512]{1,0:T(8,128)}) %reduce-scatter.2.cloned.1.call-update) | async-done | bytes 262160 | tf_op jit(solution)/shard_map/reduce_scatter | solution.py:122
  (98 shorter events, 25.6 us)
Async XLA Ops:
  7.2 22.0 %copy-start = (bf16[1,256,1024]{2,1,0:T(8,128)(2,1)S(1)}, bf16[1,256,1024]{2,1,0:T(8,128)(2,1)}, u32[]{:S(2)}) copy-start(bf16[1,256,1024]{2,1,0:T(8,128)(2,1)} %param.6) | copy-start | bytes 1572868
  7.2 15.1 %copy-start.17 = (bf16[1,256,1024]{2,1,0:T(8,128)(2,1)S(1)}, bf16[1,256,1024]{2,1,0:T(8,128)(2,1)}, u32[]{:S(2)}) copy-start(bf16[1,256,1024]{2,1,0:T(8,128)(2,1)} %param.7) | copy-start | bytes 1572868
  7.2 15.1 %copy-start.16 = (bf16[1,256,1024]{2,1,0:T(8,128)(2,1)S(1)}, bf16[1,256,1024]{2,1,0:T(8,128)(2,1)}, u32[]{:S(2)}) copy-start(bf16[1,256,1024]{2,1,0:T(8,128)(2,1)} %param.8) | copy-start | bytes 1572868
  7.2 91.4 %all-gather.6.cloned.1.call-start = ((), (), s32[]{:S(2)}) async-start(), calls=%async_computation.10 | async-start | bytes 4718592 | tf_op jit(solution)/shard_map/all_gather | solution.py:117
  12.0 178.6 %all-gather.4.cloned.1.call-start = ((), (), s32[]{:S(2)}) async-start(), calls=%async_computation.8 | async-start | bytes 4718592 | tf_op jit(solution)/shard_map/all_gather | solution.py:114
  22.3 7.4 %copy-start.18 = (s32[1,8]{1,0:T(1,128)S(1)}, s32[1,8]{1,0:T(1,128)}, u32[]{:S(2)}) copy-start(s32[1,8]{1,0:T(1,128)} %param.10) | copy-start | bytes 100
  23.4 22.9 %all-to-all-start.1 = ((bf16[128,8,128]{0,2,1:T(8,128)(2,1)}), bf16[128,8,128]{0,2,1:T(8,128)(2,1)S(1)}, u32[]{:S(2)}, u32[]{:S(2)}) async-start(bf16[128,8,128]{0,2,1:T(8,128)(2,1)} %bitcast.9), calls=%async_computation.1 | async-start | bytes 524288 | tf_op jit(solution)/shard_map/all_to_all | solution.py:75
  46.3 16.6 %all-to-all-start = ((bf16[128,8,128]{0,2,1:T(8,128)(2,1)}), bf16[128,8,128]{0,2,1:T(8,128)(2,1)S(1)}, u32[]{:S(2)}, u32[]{:S(2)}) async-start(bf16[128,8,128]{0,2,1:T(8,128)(2,1)} %bitcast.6), calls=%async_computation | async-start | bytes 524288 | tf_op jit(solution)/shard_map/all_to_all | solution.py:74
  62.8 21.9 %all-to-all-start.2 = ((bf16[128,8,128]{0,2,1:T(8,128)(2,1)}), bf16[128,8,128]{0,2,1:T(8,128)(2,1)S(1)}, u32[]{:S(2)}, u32[]{:S(2)}) async-start(bf16[128,8,128]{0,2,1:T(8,128)(2,1)} %bitcast.12), calls=%async_computation.2 | async-start | bytes 524288 | tf_op jit(solution)/shard_map/all_to_all | solution.py:76
  68.7 18.6 %copy-start.6 = (bf16[4,128,128]{2,1,0:T(8,128)(2,1)}, bf16[4,128,128]{2,1,0:T(8,128)(2,1)S(1)}, u32[]{:S(2)}) copy-start(bf16[4,128,128]{2,1,0:T(8,128)(2,1)S(1)} %copy.26) | copy-start | bytes 393220
  68.9 18.4 %copy-start.14 = (bf16[4,128,128]{2,1,0:T(8,128)(2,1)}, bf16[4,128,128]{2,1,0:T(8,128)(2,1)S(1)}, u32[]{:S(2)}) copy-start(bf16[4,128,128]{2,1,0:T(8,128)(2,1)S(1)} %copy.21) | copy-start | bytes 393220
  98.6 3.7 %copy-start.1 = (f32[512,1024]{1,0:T(8,128)S(1)}, f32[512,1024]{1,0:T(8,128)}, u32[]{:S(2)}) copy-start(f32[512,1024]{1,0:T(8,128)} %get-tuple-element.13) | copy-start | bytes 6291460
  104.0 21.0 %all-to-all-start.6 = ((bf16[8,128,128]{2,1,0:T(8,128)(2,1)}), bf16[8,128,128]{2,1,0:T(8,128)(2,1)}, u32[]{:S(2)}, u32[]{:S(2)}) async-start(bf16[8,128,128]{2,1,0:T(8,128)(2,1)} %bitcast.79), calls=%async_computation.6 | async-start | bytes 524288 | tf_op jit(solution)/shard_map/all_to_all | solution.py:151
  108.1 109.4 %reduce-scatter.2.cloned.1.call-start = ((), (), s32[]{:S(2)}) async-start(), calls=%async_computation.9 | async-start | bytes 1310720 | tf_op jit(solution)/shard_map/reduce_scatter | solution.py:122
  110.4 2.9 %copy-start.8 = (bf16[512,128]{1,0:T(8,128)(2,1)}, bf16[512,128]{1,0:T(8,128)(2,1)S(1)}, u32[]{:S(2)}) copy-start(bf16[512,128]{1,0:T(8,128)(2,1)S(1)} %get-tuple-element.22) | copy-start | bytes 393220
  110.4 2.9 %copy-start.5 = (bf16[1,1024,2048]{2,1,0:T(8,128)(2,1)S(1)}, bf16[1,1024,2048]{2,1,0:T(8,128)(2,1)}, u32[]{:S(2)}) copy-start(bf16[1,1024,2048]{2,1,0:T(8,128)(2,1)} %all-gather.6.cloned.1.call-done) | copy-start | bytes 12582916
  125.1 14.0 %all-to-all-start.5 = ((bf16[8,128,128]{2,1,0:T(8,128)(2,1)}), bf16[8,128,128]{2,1,0:T(8,128)(2,1)S(1)}, u32[]{:S(2)}, u32[]{:S(2)}) async-start(bf16[8,128,128]{2,1,0:T(8,128)(2,1)} %bitcast.25), calls=%async_computation.5 | async-start | bytes 524288 | tf_op jit(solution)/shard_map/all_to_all | solution.py:150
  128.7 13.8 %copy-start.9 = (bf16[512,128]{1,0:T(8,128)(2,1)S(1)}, bf16[512,128]{1,0:T(8,128)(2,1)}, u32[]{:S(2)}) copy-start(bf16[512,128]{1,0:T(8,128)(2,1)} %copy-done.8) | copy-start | bytes 393220
  139.0 20.0 %all-to-all-start.4 = ((bf16[8,128,128]{2,1,0:T(8,128)(2,1)}), bf16[8,128,128]{2,1,0:T(8,128)(2,1)S(1)}, u32[]{:S(2)}, u32[]{:S(2)}) async-start(bf16[8,128,128]{2,1,0:T(8,128)(2,1)} %bitcast.23), calls=%async_computation.4 | async-start | bytes 524288 | tf_op jit(solution)/shard_map/all_to_all | solution.py:149
  159.0 31.6 %all-to-all-start.3 = ((bf16[8,128,128]{1,2,0:T(8,128)(2,1)}), bf16[8,128,128]{1,2,0:T(8,128)(2,1)S(1)}, u32[]{:S(2)}, u32[]{:S(2)}) async-start(bf16[8,128,128]{1,2,0:T(8,128)(2,1)} %copy.27), calls=%async_computation.3 | async-start | bytes 524288 | tf_op jit(solution)/shard_map/all_to_all | solution.py:112
  166.0 27.5 %copy-start.11 = (bf16[1,256,1024]{2,1,0:T(8,128)(2,1)}, bf16[1,256,1024]{2,1,0:T(8,128)(2,1)S(1)}, u32[]{:S(2)}) copy-start(bf16[1,256,1024]{2,1,0:T(8,128)(2,1)S(1)} %dynamic_update_slice.15) | copy-start | bytes 1572868
  167.4 26.0 %copy-start.12 = (bf16[1,256,1024]{2,1,0:T(8,128)(2,1)}, bf16[1,256,1024]{2,1,0:T(8,128)(2,1)S(1)}, u32[]{:S(2)}) copy-start(bf16[1,256,1024]{2,1,0:T(8,128)(2,1)S(1)} %dynamic_update_slice.14) | copy-start | bytes 1572868
  168.9 21.6 %copy-start.13 = (bf16[1,256,1024]{2,1,0:T(8,128)(2,1)}, bf16[1,256,1024]{2,1,0:T(8,128)(2,1)S(1)}, u32[]{:S(2)}) copy-start(bf16[1,256,1024]{2,1,0:T(8,128)(2,1)S(1)} %dynamic_update_slice.13) | copy-start | bytes 1572868
  196.1 21.3 %copy-start.10 = (bf16[1,256,2048]{2,1,0:T(8,128)(2,1)}, bf16[1,256,2048]{2,1,0:T(8,128)(2,1)S(1)}, u32[]{:S(2)}) copy-start(bf16[1,256,2048]{2,1,0:T(8,128)(2,1)S(1)} %dynamic_update_slice.12) | copy-start | bytes 3145732
  (5 other events, 8.4 us)
Sparse Core Ops, SparseCore 0:
  12.1 86.5 all-gather.5
  100.8 89.7 all-gather.3
  193.6 23.7 reduce-scatter.1
where the time goes:
time: 225 us; the launch traced here: 224 us
  waiting for transfers between devices  123 us (55%)
  starting transfers between devices  29.8 us (13%)
  matrix products  20.6 us (9%)
  between operations  15.6 us (7%)
  local copies, waits for them, and re-layouts  13.3 us (6%)
  other arithmetic  11.8 us (5%)
  blocking collectives  10.2 us (5%)
    all_gather x1, waiting for transfers between devices, shards(): full_proj = lax.all_gather(head_rows, 'ctx', axis=0, tiled=True)  21.6 us
    reduce_scatter x1, waiting for transfers between devices, shards(): lax.psum_scatter(weight_term, 'dp', scatter_dimension=1, tiled=True)  21.3 us
    all_to_all x1, waiting for transfers between devices, shards(): lax.all_to_all(v_slot, 'ctx', split_axis=1, concat_axis=0, tiled=True)  15.9 us
    all_to_all x1, waiting for transfers between devices, shards(): lax.all_to_all(k_slot, 'ctx', split_axis=1, concat_axis=0, tiled=True)  15.6 us
    all_to_all x1, waiting for transfers between devices, shards(): lax.all_to_all(q_heads_grad, 'ctx', split_axis=0, concat_axis=1, tiled=True)  15.6 us
    all_to_all x1, waiting for transfers between devices, shards(): lax.all_to_all(q_slot, 'ctx', split_axis=1, concat_axis=0, tiled=True)  12.3 us
    all_gather x1, blocking collectives, shards(): head_rows = lax.all_gather(proj, 'dp', axis=1, tiled=True)  10.2 us
    dot_general x5, matrix products, cross_dot(): lax.dot_general(left_op, right_op, (((1,), (1,)), ((), ())), preferred_el...  8.94 us
  transfers between devices with their start and end apart: 10, of which 9 were waited for; matrix products, arithmetic and copies ran while one was open for 19% of the time, Pallas kernels for 0%

commit v1 on v0

--- a/solution.py
+++ b/solution.py
@@ -146,7 +146,12 @@
     k_heads_grad = (key_grad * score_scale).astype(jnp.bfloat16)
     v_heads_grad = value_grad.astype(jnp.bfloat16)
     q_back, k_back, v_back = (
-        lax.all_to_all(q_heads_grad, "ctx", split_axis=0, concat_axis=1, tiled=True),
+        jnp.concatenate(
+            lax.all_to_all(
+                jnp.stack(jnp.split(q_heads_grad, lax.axis_size("ctx"), axis=0)), "ctx", 0, 0
+            ),
+            axis=1,
+        ),
         lax.all_to_all(k_heads_grad, "ctx", split_axis=0, concat_axis=1, tiled=True),
         lax.all_to_all(v_heads_grad, "ctx", split_axis=0, concat_axis=1, tiled=True),
     )

time: 225 us -> 227 us (level)
  local copies, waits for them, and re-layouts: 13.3 us -> 21.2 us
  matrix products: 20.6 us -> 16.8 us
  blocking collectives: 10.2 us -> 7.62 us
    all_gather x1, waiting for transfers between devices: 4.03 us -> 16.9 us  [shards(): part_rows = lax.all_gather(g_slot, 'ctx', axis=0, tiled=True)]
    all_to_all x1, waiting for transfers between devices: 15.6 us -> 5.75 us  [shards(): lax.all_to_all(k_slot, 'ctx', split_axis=1, concat_axis=0, tiled=True)]
    unnamed x41 -> x48, local copies, waits for them, and re-layouts: 1.31 us -> 7.58 us
    all_gather x1, blocking collectives: 10.2 us -> 7.62 us  [shards(): head_rows = lax.all_gather(proj, 'dp', axis=1, tiled=True)]
where the time goes in v1:
time: 227 us; the launch traced here: 226 us
  waiting for transfers between devices  123 us (54%)
  starting transfers between devices  30.8 us (14%)
  local copies, waits for them, and re-layouts  21.2 us (9%)
  matrix products  16.8 us (7%)
  between operations  15.6 us (7%)
  other arithmetic  10.1 us (4%)
  blocking collectives  7.62 us (3%)
    all_gather x1, waiting for transfers between devices, shards(): full_proj = lax.all_gather(head_rows, 'ctx', axis=0, tiled=True)  22.1 us
    reduce_scatter x1, waiting for transfers between devices, shards(): lax.psum_scatter(weight_term, 'dp', scatter_dimension=1, tiled=True)  21.3 us
    all_gather x1, waiting for transfers between devices, shards(): part_rows = lax.all_gather(g_slot, 'ctx', axis=0, tiled=True)  16.9 us
    all_to_all x1, waiting for transfers between devices, shards(): lax.all_to_all(jnp.stack(jnp.split(q_heads_grad, lax.axis_size('ctx'), ax...  15.8 us
    all_to_all x1, waiting for transfers between devices, shards(): lax.all_to_all(v_slot, 'ctx', split_axis=1, concat_axis=0, tiled=True)  15.2 us
    all_to_all x1, waiting for transfers between devices, shards(): lax.all_to_all(q_slot, 'ctx', split_axis=1, concat_axis=0, tiled=True)  11.3 us
    all_to_all x1, waiting for transfers between devices, shards(): lax.all_to_all(k_heads_grad, 'ctx', split_axis=0, concat_axis=1, tiled=True)  9.75 us
    all_gather x1, blocking collectives, shards(): head_rows = lax.all_gather(proj, 'dp', axis=1, tiled=True)  7.62 us
  transfers between devices with their start and end apart: 10, of which 9 were waited for; matrix products, arithmetic and copies ran while one was open for 19% of the time, Pallas kernels for 0%

profile of v1, /device:TPU:0, one launch (start us, length us, event | category | flops | bytes accessed | tf_op | source)
XLA Modules:
  0.0 225.6 jit_solution(16885216155797415011)
XLA Ops:
  9.9 2.0 dynamic-slice_select_fusion
  14.0 7.3 %all-to-all-start.1 = ((bf16[128,8,128]{0,2,1:T(8,128)(2,1)}), bf16[128,8,128]{0,2,1:T(8,128)(2,1)S(1)}, u32[]{:S(2)}, u32[]{:S(2)}) async-start(bf16[128,8,128]{0,2,1:T(8,128)(2,1)} %bitcast.9), calls=%async_computation.1 | async-start | bytes 524288 | tf_op jit(solution)/shard_map/all_to_all | solution.py:75
  21.4 7.6 %all_gather.9 = bf16[128,2048]{1,0:T(8,128)(2,1)} all-gather(bf16[128,512]{1,0:T(8,128)(2,1)S(1)} %copy-done.17), channel_id=1, replica_groups=mesh['dp'=4,'ctx'=8] {'dp'}, dimensions={1}, use_global_device_ids=true | all-gather | bytes 655360 | tf_op jit(solution)/shard_map/all_gather | solution.py:113
  30.5 5.7 %all-to-all-done.1 = bf16[128,8,128]{0,2,1:T(8,128)(2,1)S(1)} async-done(((bf16[128,8,128]{0,2,1:T(8,128)(2,1)}), bf16[128,8,128]{0,2,1:T(8,128)(2,1)S(1)}, u32[]{:S(2)}, u32[]{:S(2)}) %all-to-all-start.1) | async-done | bytes 262176 | tf_op jit(solution)/shard_map/all_to_all | solution.py:75
  36.2 4.4 %all-to-all-start = ((bf16[128,8,128]{0,2,1:T(8,128)(2,1)}), bf16[128,8,128]{0,2,1:T(8,128)(2,1)S(1)}, u32[]{:S(2)}, u32[]{:S(2)}) async-start(bf16[128,8,128]{0,2,1:T(8,128)(2,1)} %bitcast.6), calls=%async_computation | async-start | bytes 524288 | tf_op jit(solution)/shard_map/all_to_all | solution.py:74
  41.5 11.3 %all-to-all-done = bf16[128,8,128]{0,2,1:T(8,128)(2,1)S(1)} async-done(((bf16[128,8,128]{0,2,1:T(8,128)(2,1)}), bf16[128,8,128]{0,2,1:T(8,128)(2,1)S(1)}, u32[]{:S(2)}, u32[]{:S(2)}) %all-to-all-start) | async-done | bytes 262176 | tf_op jit(solution)/shard_map/all_to_all | solution.py:74
  52.7 3.6 %all-to-all-start.2 = ((bf16[128,8,128]{0,2,1:T(8,128)(2,1)}), bf16[128,8,128]{0,2,1:T(8,128)(2,1)S(1)}, u32[]{:S(2)}, u32[]{:S(2)}) async-start(bf16[128,8,128]{0,2,1:T(8,128)(2,1)} %bitcast.12), calls=%async_computation.2 | async-start | bytes 524288 | tf_op jit(solution)/shard_map/all_to_all | solution.py:76
  56.9 15.2 %all-to-all-done.2 = bf16[128,8,128]{0,2,1:T(8,128)(2,1)S(1)} async-done(((bf16[128,8,128]{0,2,1:T(8,128)(2,1)}), bf16[128,8,128]{0,2,1:T(8,128)(2,1)S(1)}, u32[]{:S(2)}, u32[]{:S(2)}) %all-to-all-start.2) | async-done | bytes 262176 | tf_op jit(solution)/shard_map/all_to_all | solution.py:76
  72.7 1.9 fusion.7
  74.6 3.0 %fusion.11 = (f32[512]{0:T(512)S(1)}, f32[512]{0:T(512)S(1)}) fusion(f32[512,1024]{1,0:T(8,128)S(1)} %get-tuple-element.21, f32[512]{0:T(512)S(1)} %get-tuple-element.9, s32[512]{0:T(512)S(1)} %slice.46, s32[512]{0:T(512)S(1)} %get-tuple-element.16, s32[1024]{0:T(1024)S(1)} %get-tuple-element.19, pred[1024]{0:T(1024)(128)(4,1)S(1)} %broadcast_bitcast_fusion, ...), kind=kLoop, calls=%fused_computation.22 | loop fusion | flops 10484736 | bytes 4216832 | tf_op jit(solution)/shard_map/reduce_sum | solution.py:40
  77.6 2.8 %fusion.10 = (f32[512,1024]{1,0:T(8,128)S(1)}, f32[512,1024]{1,0:T(8,128)S(1)}) fusion(f32[512,1024]{1,0:T(8,128)S(1)} %get-tuple-element.21, f32[512]{0:T(512)S(1)} %get-tuple-element.7, f32[512]{0:T(512)S(1)} %get-tuple-element.9, s32[512]{0:T(512)S(1)} %slice.46, s32[512]{0:T(512)S(1)} %get-tuple-element.16, s32[1024]{0:T(1024)S(1)} %get-tuple-element.19, ...), kind=kLoop, calls=%fused_computation.21 | loop fusion | flops 10485760 | bytes 8411136 | tf_op jit(solution)/shard_map/div | solution.py:40
  82.2 16.9 %all-gather.6.cloned.1.call-done = bf16[1,1024,2048]{2,1,0:T(8,128)(2,1)} async-done(((bf16[1,128,2048]{2,1,0:T(8,128)(2,1)}), bf16[1,1024,2048]{2,1,0:T(8,128)(2,1)}) %all-gather.6.cloned.1.call-update) | async-done | bytes 4194320 | tf_op jit(solution)/shard_map/all_gather | solution.py:117
  99.2 3.7 %fusion.16 = bf16[1024,128]{1,0:T(8,128)(2,1)S(1)} fusion(bf16[128,2048]{1,0:T(8,128)(2,1)} %all_gather.9, bf16[1,1024,2048]{2,1,0:T(8,128)(2,1)} %all-gather.6.cloned.1.call-done), kind=kOutput, calls=%fused_computation.27 | convolution fusion | flops 537001984 | bytes 4980736 | tf_op jit(solution)/shard_map/dot_general | solution.py:11
  104.6 4.0 %all-to-all-start.6 = ((bf16[8,128,128]{2,1,0:T(8,128)(2,1)}), bf16[8,128,128]{2,1,0:T(8,128)(2,1)}, u32[]{:S(2)}, u32[]{:S(2)}) async-start(bf16[8,128,128]{2,1,0:T(8,128)(2,1)} %bitcast.110), calls=%async_computation.6 | async-start | bytes 524288 | tf_op jit(solution)/shard_map/all_to_all | solution.py:156
  119.1 5.4 %all-to-all-done.6 = bf16[8,128,128]{2,1,0:T(8,128)(2,1)} async-done(((bf16[8,128,128]{2,1,0:T(8,128)(2,1)}), bf16[8,128,128]{2,1,0:T(8,128)(2,1)}, u32[]{:S(2)}, u32[]{:S(2)}) %all-to-all-start.6) | async-done | bytes 262176 | tf_op jit(solution)/shard_map/all_to_all | solution.py:156
  124.5 4.1 %all-to-all-start.5 = ((bf16[8,128,128]{2,1,0:T(8,128)(2,1)}), bf16[8,128,128]{2,1,0:T(8,128)(2,1)S(1)}, u32[]{:S(2)}, u32[]{:S(2)}) async-start(bf16[8,128,128]{2,1,0:T(8,128)(2,1)} %bitcast.33), calls=%async_computation.5 | async-start | bytes 524288 | tf_op jit(solution)/shard_map/all_to_all | solution.py:155
  130.4 9.8 %all-to-all-done.5 = bf16[8,128,128]{2,1,0:T(8,128)(2,1)S(1)} async-done(((bf16[8,128,128]{2,1,0:T(8,128)(2,1)}), bf16[8,128,128]{2,1,0:T(8,128)(2,1)S(1)}, u32[]{:S(2)}, u32[]{:S(2)}) %all-to-all-start.5) | async-done | bytes 262176 | tf_op jit(solution)/shard_map/all_to_all | solution.py:155
  140.2 3.6 %all-to-all-start.4 = ((bf16[8,128,128]{2,1,0:T(8,128)(2,1)}), bf16[8,128,128]{2,1,0:T(8,128)(2,1)S(1)}, u32[]{:S(2)}, u32[]{:S(2)}) async-start(bf16[8,128,128]{2,1,0:T(8,128)(2,1)} %fusion.30), calls=%async_computation.4 | async-start | bytes 524288 | tf_op jit(solution)/shard_map/all_to_all | solution.py:150
  144.7 15.8 %all-to-all-done.4 = bf16[8,128,128]{2,1,0:T(8,128)(2,1)S(1)} async-done(((bf16[8,128,128]{2,1,0:T(8,128)(2,1)}), bf16[8,128,128]{2,1,0:T(8,128)(2,1)S(1)}, u32[]{:S(2)}, u32[]{:S(2)}) %all-to-all-start.4) | async-done | bytes 262176 | tf_op jit(solution)/shard_map/all_to_all | solution.py:150
  160.5 3.4 %all-to-all-start.3 = ((bf16[8,128,128]{1,2,0:T(8,128)(2,1)}), bf16[8,128,128]{1,2,0:T(8,128)(2,1)S(1)}, u32[]{:S(2)}, u32[]{:S(2)}) async-start(bf16[8,128,128]{1,2,0:T(8,128)(2,1)} %copy.27), calls=%async_computation.3 | async-start | bytes 524288 | tf_op jit(solution)/shard_map/all_to_all | solution.py:112
  170.1 22.1 %all-gather.4.cloned.1.call-done = bf16[1024,2048]{1,0:T(8,128)(2,1)} async-done(((bf16[128,2048]{1,0:T(8,128)(2,1)}), bf16[1024,2048]{1,0:T(8,128)(2,1)}) %all-gather.4.cloned.1.call-update) | async-done | bytes 4194320 | tf_op jit(solution)/shard_map/all_gather | solution.py:114
  192.2 2.9 %fusion.4 = bf16[1,128,2048]{2,1,0:T(8,128)(2,1)S(1)} fusion(bf16[128,1024]{0,1:T(8,128)(2,1)S(1)} %bitcast.111, bf16[1024,2048]{1,0:T(8,128)(2,1)} %all-gather.4.cloned.1.call-done), kind=kOutput, calls=%fused_computation.5 | convolution fusion | flops 537133056 | bytes 4980736 | tf_op jit(solution)/shard_map/dot_general | solution.py:115
  195.3 2.5 %dynamic_update_slice.12 = bf16[1,256,2048]{2,1,0:T(8,128)(2,1)S(1)} dynamic-update-slice(bf16[1,256,2048]{2,1,0:T(8,128)(2,1)S(1)} %broadcast_in_dim.56, bf16[1,128,2048]{2,1,0:T(8,128)(2,1)S(1)} %fusion.4, s32[]{:T(128)} %constant.48.clone.1, s32[]{:T(128)S(6)} %select_n.105, s32[]{:T(128)} %constant.48.clone.1) | dynamic-update-slice | bytes 1048580 | tf_op jit(solution)/shard_map/dynamic_update_slice | solution.py:65
  197.8 21.3 %reduce-scatter.2.cloned.1.call-done = f32[128,512]{1,0:T(8,128)} async-done(((f32[128,2048]{1,0:T(8,128)}), f32[128,512]{1,0:T(8,128)}) %reduce-scatter.2.cloned.1.call-update) | async-done | bytes 262160 | tf_op jit(solution)/shard_map/reduce_scatter | solution.py:122
  (105 shorter events, 29.6 us)
Async XLA Ops:
  7.2 21.9 %copy-start = (bf16[1,256,1024]{2,1,0:T(8,128)(2,1)S(1)}, bf16[1,256,1024]{2,1,0:T(8,128)(2,1)}, u32[]{:S(2)}) copy-start(bf16[1,256,1024]{2,1,0:T(8,128)(2,1)} %param.6) | copy-start | bytes 1572868
  7.2 92.0 %all-gather.6.cloned.1.call-start = ((), (), s32[]{:S(2)}) async-start(), calls=%async_computation.10 | async-start | bytes 4718592 | tf_op jit(solution)/shard_map/all_gather | solution.py:117
  9.9 11.5 %copy-start.17 = (bf16[128,512]{1,0:T(8,128)(2,1)S(1)}, bf16[128,512]{1,0:T(8,128)(2,1)}, u32[]{:S(2)}) copy-start(bf16[128,512]{1,0:T(8,128)(2,1)} %param.11) | copy-start | bytes 393220
  11.9 17.1 %copy-start.18 = (s32[1,8]{1,0:T(1,128)S(1)}, s32[1,8]{1,0:T(1,128)}, u32[]{:S(2)}) copy-start(s32[1,8]{1,0:T(1,128)} %param.10) | copy-start | bytes 100
  14.0 22.2 %all-to-all-start.1 = ((bf16[128,8,128]{0,2,1:T(8,128)(2,1)}), bf16[128,8,128]{0,2,1:T(8,128)(2,1)S(1)}, u32[]{:S(2)}, u32[]{:S(2)}) async-start(bf16[128,8,128]{0,2,1:T(8,128)(2,1)} %bitcast.9), calls=%async_computation.1 | async-start | bytes 524288 | tf_op jit(solution)/shard_map/all_to_all | solution.py:75
  21.4 170.8 %all-gather.4.cloned.1.call-start = ((), (), s32[]{:S(2)}) async-start(), calls=%async_computation.8 | async-start | bytes 4718592 | tf_op jit(solution)/shard_map/all_gather | solution.py:114
  36.2 16.5 %all-to-all-start = ((bf16[128,8,128]{0,2,1:T(8,128)(2,1)}), bf16[128,8,128]{0,2,1:T(8,128)(2,1)S(1)}, u32[]{:S(2)}, u32[]{:S(2)}) async-start(bf16[128,8,128]{0,2,1:T(8,128)(2,1)} %bitcast.6), calls=%async_computation | async-start | bytes 524288 | tf_op jit(solution)/shard_map/all_to_all | solution.py:74
  52.7 19.3 %all-to-all-start.2 = ((bf16[128,8,128]{0,2,1:T(8,128)(2,1)}), bf16[128,8,128]{0,2,1:T(8,128)(2,1)S(1)}, u32[]{:S(2)}, u32[]{:S(2)}) async-start(bf16[128,8,128]{0,2,1:T(8,128)(2,1)} %bitcast.12), calls=%async_computation.2 | async-start | bytes 524288 | tf_op jit(solution)/shard_map/all_to_all | solution.py:76
  56.7 17.9 %copy-start.5 = (bf16[4,128,128]{2,1,0:T(8,128)(2,1)}, bf16[4,128,128]{2,1,0:T(8,128)(2,1)S(1)}, u32[]{:S(2)}) copy-start(bf16[4,128,128]{2,1,0:T(8,128)(2,1)S(1)} %copy.26) | copy-start | bytes 393220
  56.9 17.7 %copy-start.15 = (bf16[4,128,128]{2,1,0:T(8,128)(2,1)}, bf16[4,128,128]{2,1,0:T(8,128)(2,1)S(1)}, u32[]{:S(2)}) copy-start(bf16[4,128,128]{2,1,0:T(8,128)(2,1)S(1)} %copy.21) | copy-start | bytes 393220
  99.2 3.7 %copy-start.2 = (f32[512,1024]{1,0:T(8,128)S(1)}, f32[512,1024]{1,0:T(8,128)}, u32[]{:S(2)}) copy-start(f32[512,1024]{1,0:T(8,128)} %copy-done.1) | copy-start | bytes 6291460
  104.6 20.0 %all-to-all-start.6 = ((bf16[8,128,128]{2,1,0:T(8,128)(2,1)}), bf16[8,128,128]{2,1,0:T(8,128)(2,1)}, u32[]{:S(2)}, u32[]{:S(2)}) async-start(bf16[8,128,128]{2,1,0:T(8,128)(2,1)} %bitcast.110), calls=%async_computation.6 | async-start | bytes 524288 | tf_op jit(solution)/shard_map/all_to_all | solution.py:156
  108.6 110.5 %reduce-scatter.2.cloned.1.call-start = ((), (), s32[]{:S(2)}) async-start(), calls=%async_computation.9 | async-start | bytes 1310720 | tf_op jit(solution)/shard_map/reduce_scatter | solution.py:122
  109.4 6.0 %copy-start.7 = (bf16[512,128]{1,0:T(8,128)(2,1)}, bf16[512,128]{1,0:T(8,128)(2,1)S(1)}, u32[]{:S(2)}) copy-start(bf16[512,128]{1,0:T(8,128)(2,1)S(1)} %get-tuple-element.22) | copy-start | bytes 393220
  113.2 2.2 copy-start.4
  115.4 1.8 copy-start.14
  117.2 26.6 %copy-start.8 = (bf16[512,128]{1,0:T(8,128)(2,1)S(1)}, bf16[512,128]{1,0:T(8,128)(2,1)}, u32[]{:S(2)}) copy-start(bf16[512,128]{1,0:T(8,128)(2,1)} %copy-done.7) | copy-start | bytes 393220
  124.5 15.7 %all-to-all-start.5 = ((bf16[8,128,128]{2,1,0:T(8,128)(2,1)}), bf16[8,128,128]{2,1,0:T(8,128)(2,1)S(1)}, u32[]{:S(2)}, u32[]{:S(2)}) async-start(bf16[8,128,128]{2,1,0:T(8,128)(2,1)} %bitcast.33), calls=%async_computation.5 | async-start | bytes 524288 | tf_op jit(solution)/shard_map/all_to_all | solution.py:155
  140.2 20.3 %all-to-all-start.4 = ((bf16[8,128,128]{2,1,0:T(8,128)(2,1)}), bf16[8,128,128]{2,1,0:T(8,128)(2,1)S(1)}, u32[]{:S(2)}, u32[]{:S(2)}) async-start(bf16[8,128,128]{2,1,0:T(8,128)(2,1)} %fusion.30), calls=%async_computation.4 | async-start | bytes 524288 | tf_op jit(solution)/shard_map/all_to_all | solution.py:150
  160.5 31.7 %all-to-all-start.3 = ((bf16[8,128,128]{1,2,0:T(8,128)(2,1)}), bf16[8,128,128]{1,2,0:T(8,128)(2,1)S(1)}, u32[]{:S(2)}, u32[]{:S(2)}) async-start(bf16[8,128,128]{1,2,0:T(8,128)(2,1)} %copy.27), calls=%async_computation.3 | async-start | bytes 524288 | tf_op jit(solution)/shard_map/all_to_all | solution.py:112
  167.2 27.9 %copy-start.10 = (bf16[1,256,1024]{2,1,0:T(8,128)(2,1)}, bf16[1,256,1024]{2,1,0:T(8,128)(2,1)S(1)}, u32[]{:S(2)}) copy-start(bf16[1,256,1024]{2,1,0:T(8,128)(2,1)S(1)} %dynamic_update_slice.15) | copy-start | bytes 1572868
  168.7 26.5 %copy-start.11 = (bf16[1,256,1024]{2,1,0:T(8,128)(2,1)}, bf16[1,256,1024]{2,1,0:T(8,128)(2,1)S(1)}, u32[]{:S(2)}) copy-start(bf16[1,256,1024]{2,1,0:T(8,128)(2,1)S(1)} %dynamic_update_slice.14) | copy-start | bytes 1572868
  170.1 22.1 %copy-start.12 = (bf16[1,256,1024]{2,1,0:T(8,128)(2,1)}, bf16[1,256,1024]{2,1,0:T(8,128)(2,1)S(1)}, u32[]{:S(2)}) copy-start(bf16[1,256,1024]{2,1,0:T(8,128)(2,1)S(1)} %dynamic_update_slice.13) | copy-start | bytes 1572868
  197.8 21.3 %copy-start.9 = (bf16[1,256,2048]{2,1,0:T(8,128)(2,1)}, bf16[1,256,2048]{2,1,0:T(8,128)(2,1)S(1)}, u32[]{:S(2)}) copy-start(bf16[1,256,2048]{2,1,0:T(8,128)(2,1)S(1)} %dynamic_update_slice.12) | copy-start | bytes 3145732
  (5 other events, 6.7 us)
Sparse Core Ops, SparseCore 0:
  12.1 87.0 all-gather.5
  101.3 90.8 all-gather.3
  195.3 23.7 reduce-scatter.1
